TPU v7x, 512 devices: a whole 4x4x16 slice. The times are simulated.
512 devices in a mesh: slab: 128 (over z, x, core), img: 4 (over y).
Axes of the slice: x: 4, y: 4, z: 16, core: 2. Of those that a mesh axis runs over, the one named last changes fastest.
Arguments:
- images: bfloat16 [65536, 2, 4, 512], P(('slab', 'img')), may hold values from -6 to 6
- pose_bins: int32 [65536], P(('slab', 'img')), may hold values from 0 to 8191, as said below
- labels: int32 [65536], P(('slab', 'img')), may hold values from 0 to 1
- defocus: bfloat16 [65536], P(('slab', 'img')), may hold values from 0.5 to 2
Outputs:
- maps: float32 [4, 1024, 2, 512], P('img', 'slab')
Inputs may be any that keep to these rules, and one draw needn't show every extreme that they name: With owner = (pose_bins // 16) // 4: among the 128 images of one device (aligned blocks in order), no owner is named more than 2 times, and one owner, the same for all blocks, is named exactly 2 times in every block.
All inputs are finite; a program needn't handle non-finite values.
Results may differ from a plain program's by a relative error of at most 0.025.
Values may be sent and summed in bfloat16 or wider, within the bound.
A program may use at most 64 MiB of HBM per device.

v0:
```python
import math

import jax
import jax.numpy as jnp
import ml_dtypes
import numpy as np
from jax import lax
from jax.experimental import pallas as pl
from jax.experimental.pallas import tpu as pltpu
from jax.sharding import PartitionSpec as P

NX = 512
KY = 4
NZ = 512
CLASSES = 2
ZBINS = 4
XBINS = 4
TAPS = 8
IMG_DEV = 128
IMAGES = 65536

ZC = 16
Q = 8
NY = 4
J = NX * CLASSES // (ZC * Q)
K = NX // (Q * J)
PLANE = NY * Q

MESH = pl.DeviceIdType.MESH


def tap_values(bins):
    fraction = (np.arange(bins) + 0.5) / bins
    distance = np.arange(TAPS)[None, :] - 3.0 - fraction[:, None]
    kernel = np.sinc(distance) * np.sinc(distance / 4.0)
    kernel = kernel / kernel.sum(axis=-1, keepdims=True)
    return kernel.astype(np.float32).astype(ml_dtypes.bfloat16).astype(np.float64)


def column_order():
    q, r, k, j = np.meshgrid(
        np.arange(Q), np.arange(2), np.arange(K), np.arange(J), indexing="ij"
    )
    return (k * Q * J + q * J + j).reshape(-1), r.reshape(-1)


def x_table():
    column, part = column_order()
    angle = 2 * np.pi / NX * ((np.arange(NX)[:, None] * column[None, :]) % NX)
    return np.where(part[None, :] == 0, np.cos(angle), np.sin(angle)).astype(
        ml_dtypes.bfloat16
    )


def z_table():
    index = np.arange(NZ)
    angle = 2 * np.pi / NZ * ((index[:, None] * index[None, :]) % NZ)
    return np.concatenate([np.cos(angle), np.sin(angle)], 1).astype(ml_dtypes.bfloat16)


def tap_transform():
    column, _ = column_order()
    taps = tap_values(XBINS)
    shift = np.arange(TAPS) - 3
    wave = np.exp(2j * np.pi / NX * ((shift[:, None] * column[None, :]) % NX))
    spectrum = taps @ wave
    both = np.stack([spectrum.real, spectrum.imag])
    high = both.astype(np.float32).astype(ml_dtypes.bfloat16)
    low = (both - high.astype(np.float64)).astype(np.float32).astype(ml_dtypes.bfloat16)
    return np.concatenate([high, low], axis=1)


def radius_table():
    signed = (np.arange(NX) + NX // 2) % NX - NX // 2
    rows = np.arange(KY) + 1
    return (rows[:, None] ** 2 + signed[None, :] ** 2).astype(np.float32)


def sine_coefficients(terms):
    nodes = 0.25 + 0.25 * np.cos(np.pi * (np.arange(400) + 0.5) / 400)
    f = np.sqrt(nodes) * np.sqrt(0.5)
    basis = f[:, None] ** (2 * np.arange(terms)[None, :] + 1)
    scale = np.abs(basis).max(0)
    fit = np.linalg.lstsq(basis / scale, np.sin(2 * np.pi * f), rcond=None)[0]
    return [float(v) for v in fit / scale]


SINE = sine_coefficients(8)


def sine_turns(turns):
    f = turns - jnp.round(turns)
    t = f * f
    value = jnp.full_like(t, SINE[-1])
    for c in SINE[-2::-1]:
        value = value * t + c
    return value * f


def insertion_kernel(
    focus_ref,
    images_ref,
    key_ref,
    radius_ref,
    xtab_ref,
    xtap_ref,
    ztab_ref,
    out_ref,
    rows_ref,
    factor_ref,
    send_ref,
    recv_ref,
    keys_ref,
    spread_ref,
    total_ref,
    zsend_ref,
    zrecv_ref,
    send_sem,
    recv_sem,
    ksend_sem,
    krecv_sem,
    zsend_sem,
    zrecv_sem,
):
    slab = lax.axis_index("slab")
    me_y = lax.axis_index("img")
    me_z = slab // Q
    me_q = lax.rem(slab, Q)

    def plane_peer(dy, dq):
        return me_z * Q + lax.rem(me_q + dq, Q), lax.rem(me_y + dy, NY)

    def z_peer(dz):
        return lax.rem(me_z + dz, ZC) * Q + me_q, me_y

    barrier = pltpu.get_barrier_semaphore()

    @pl.loop(1, PLANE)
    def _(step):
        pl.semaphore_signal(
            barrier,
            inc=1,
            device_id=plane_peer(step // Q, lax.rem(step, Q)),
            device_id_type=MESH,
        )

    @pl.loop(1, ZC)
    def _(step):
        pl.semaphore_signal(
            barrier, inc=1, device_id=z_peer(step), device_id_type=MESH
        )

    radius = radius_ref[...]

    @pl.loop(0, IMG_DEV, unroll=4)
    def _(i):
        ctf = sine_turns(focus_ref[i] * radius + 0.1 / (2 * math.pi))
        value = jnp.concatenate(
            [ctf * images_ref[i, r].astype(jnp.float32) for r in range(2)], axis=0
        )
        for b in range(NX // 128):
            rows_ref[b, pl.ds(pl.multiple_of(i * 8, 8), 8), :] = value[
                :, b * 128 : (b + 1) * 128
            ]

    key = key_ref[...]
    xbin = jnp.broadcast_to(key & (XBINS - 1), (8, IMG_DEV))
    row = lax.broadcasted_iota(jnp.int32, (8, IMG_DEV), 0)
    chosen = jnp.where(xbin == (row & (XBINS - 1)), 1.0, 0.0).astype(jnp.float32)
    chosen = jnp.concatenate(
        [chosen, jnp.zeros((IMG_DEV - 8, IMG_DEV), jnp.float32)], axis=0
    ).T[:, :8]
    chosen = chosen.astype(jnp.bfloat16)
    for part in range(2):
        factor_ref[part] = jnp.dot(
            chosen, xtap_ref[part], preferred_element_type=jnp.float32
        )

    pl.semaphore_wait(barrier, PLANE - 1 + ZC - 1)

    own_key = pltpu.make_async_copy(key_ref, keys_ref.at[0], krecv_sem)
    own_key.start()

    @pl.loop(1, PLANE)
    def _(step):
        pltpu.make_async_remote_copy(
            src_ref=key_ref,
            dst_ref=keys_ref.at[step],
            send_sem=ksend_sem,
            recv_sem=krecv_sem,
            device_id=plane_peer(step // Q, lax.rem(step, Q)),
            device_id_type=MESH,
        ).start()

    half = NX // K

    def transform(ky):
        both = jnp.concatenate(
            [
                jnp.concatenate(
                    [
                        rows_ref[b, pl.ds(r * KY + ky, IMG_DEV, stride=8), :]
                        for b in range(NX // 128)
                    ],
                    axis=1,
                )
                for r in range(2)
            ],
            axis=0,
        ).astype(jnp.bfloat16)
        product = jnp.dot(both, xtab_ref[...], preferred_element_type=jnp.float32)
        lane = lax.broadcasted_iota(jnp.int32, (IMG_DEV, 128), 1)
        sign = jnp.where(lane < half, -1.0, 1.0).astype(jnp.float32)
        for q in range(Q):
            lanes = slice(q * 128, (q + 1) * 128)
            real, imag = product[:IMG_DEV, lanes], product[IMG_DEV:, lanes]
            turned = sign * pltpu.roll(imag, half, 1)
            turned_real = sign * pltpu.roll(real, half, 1)
            value = factor_ref[0, :, lanes] * (real + turned) + factor_ref[
                1, :, lanes
            ] * (turned_real - imag)
            send_ref[ky * Q + q] = value.astype(jnp.bfloat16)

    def send_row(dy):
        ky = lax.rem(me_y + dy, NY)
        if dy == 0:
            pltpu.make_async_copy(
                send_ref.at[ky * Q + me_q], recv_ref.at[0], recv_sem.at[0]
            ).start()

        @pl.loop(1 if dy == 0 else 0, Q)
        def _(dq):
            pltpu.make_async_remote_copy(
                src_ref=send_ref.at[ky * Q + lax.rem(me_q + dq, Q)],
                dst_ref=recv_ref.at[dy * Q + dq],
                send_sem=send_sem,
                recv_sem=recv_sem.at[dy],
                device_id=plane_peer(dy, dq),
                device_id_type=MESH,
            ).start()

    order = (2, 1, 3, 0)
    for dy in order:
        transform(lax.rem(me_y + dy, NY))
        send_row(dy)

    pltpu.make_async_copy(keys_ref, keys_ref, krecv_sem).wait()
    ztaps = tap_values(ZBINS)
    sub = lax.broadcasted_iota(jnp.int32, (16, IMG_DEV), 0)

    @pl.loop(0, PLANE)
    def _(slot):
        entry = keys_ref[slot]
        zbin = (entry >> 2) & (ZBINS - 1)
        start = (entry >> 4) & (NZ - 1)
        label = entry >> 13
        low = jnp.broadcast_to(start & 15, (16, IMG_DEV))
        offset = (sub - low) & 15
        base = jnp.broadcast_to(start >> 4, (16, IMG_DEV))
        base = (base + jnp.where(sub < low, 1, 0)) & 31
        block = base + jnp.broadcast_to(label * 32, (16, IMG_DEV))
        pattern = jnp.zeros((16, IMG_DEV), jnp.float32)
        for t in range(TAPS):
            tap = jnp.full((1, IMG_DEV), float(ztaps[0, t]), jnp.float32)
            for b in range(1, ZBINS):
                tap = jnp.where(zbin == b, float(ztaps[b, t]), tap)
            pattern = jnp.where(
                offset == t, jnp.broadcast_to(tap, (16, IMG_DEV)), pattern
            )
        lanes = pl.ds(pl.multiple_of(lax.rem(slot, Q) * IMG_DEV, IMG_DEV), IMG_DEV)
        for b in range(CLASSES * NZ // 16):
            spread_ref[slot // Q, b * 16 : (b + 1) * 16, lanes] = jnp.where(
                block == b, pattern, 0.0
            ).astype(jnp.bfloat16)

    for n, dy in enumerate(order):
        arrived = recv_ref.at[pl.ds(dy * Q, Q)]
        pltpu.make_async_copy(arrived, arrived, recv_sem.at[dy]).wait()
        part = jnp.dot(
            spread_ref[dy],
            recv_ref[dy * Q : (dy + 1) * Q].reshape(Q * IMG_DEV, 128),
            preferred_element_type=jnp.float32,
        )
        total_ref[...] = part if n == 0 else total_ref[...] + part

    volume = total_ref[...].T
    for c in range(CLASSES):
        planes = slice(c * NZ, (c + 1) * NZ)
        for k in range(K):
            zsend_ref[c * K + k] = jnp.concatenate(
                [
                    volume[r * half + k * J : r * half + (k + 1) * J, planes]
                    for r in range(2)
                ],
                axis=0,
            ).astype(jnp.bfloat16)

    pltpu.make_async_copy(zsend_ref.at[me_z], zrecv_ref.at[0], zrecv_sem).start()

    @pl.loop(1, ZC)
    def _(dz):
        pltpu.make_async_remote_copy(
            src_ref=zsend_ref.at[lax.rem(me_z + dz, ZC)],
            dst_ref=zrecv_ref.at[dz],
            send_sem=zsend_sem,
            recv_sem=zrecv_sem,
            device_id=z_peer(dz),
            device_id_type=MESH,
        ).start()

    pltpu.make_async_copy(zrecv_ref, zrecv_ref, zrecv_sem).wait()

    columns = jnp.zeros((2 * J, NZ), jnp.float32)
    for dz in range(ZC):
        columns = columns + zrecv_ref[dz].astype(jnp.float32)
    high = columns.astype(jnp.bfloat16)
    low = (columns - high.astype(jnp.float32)).astype(jnp.bfloat16)
    waves = jnp.dot(
        jnp.concatenate([high, low], axis=0),
        ztab_ref[...],
        preferred_element_type=jnp.float32,
    )
    waves = (waves[: 2 * J] + waves[2 * J :]) * (2.5 / math.sqrt(IMAGES * NX))
    out_ref[0] = waves[:J, :NZ] - waves[J:, NZ:]
    out_ref[1] = waves[:J, NZ:] + waves[J:, :NZ]

    plane_sent = send_ref.at[pl.ds(0, PLANE - 1)]
    pltpu.make_async_copy(plane_sent, plane_sent, send_sem).wait()
    keys_sent = keys_ref.at[pl.ds(0, PLANE - 1)]
    pltpu.make_async_copy(keys_sent, keys_sent, ksend_sem).wait()
    z_sent = zsend_ref.at[pl.ds(0, ZC - 1)]
    pltpu.make_async_copy(z_sent, z_sent, zsend_sem).wait()


def on_device(images, pose_bins, labels, defocus):
    key = (labels * (NZ * ZBINS * XBINS) + pose_bins).reshape(1, IMG_DEV)
    focus = defocus.astype(jnp.float32) * (200.0 / (NX * NX))
    vmem = pl.BlockSpec(memory_space=pltpu.VMEM)
    out = pl.pallas_call(
        insertion_kernel,
        out_shape=jax.ShapeDtypeStruct((2, J, NZ), jnp.float32),
        in_specs=[pl.BlockSpec(memory_space=pltpu.SMEM)] + [vmem] * 6,
        out_specs=vmem,
        scratch_shapes=[
            pltpu.VMEM((NX // 128, IMG_DEV * 8, 128), jnp.float32),
            pltpu.VMEM((2, IMG_DEV, 2 * NX), jnp.float32),
            pltpu.VMEM((PLANE, IMG_DEV, 128), jnp.bfloat16),
            pltpu.VMEM((PLANE, IMG_DEV, 128), jnp.bfloat16),
            pltpu.VMEM((PLANE, 1, IMG_DEV), jnp.int32),
            pltpu.VMEM((NY, CLASSES * NZ, Q * IMG_DEV), jnp.bfloat16),
            pltpu.VMEM((CLASSES * NZ, 128), jnp.float32),
            pltpu.VMEM((ZC, 2 * J, NZ), jnp.bfloat16),
            pltpu.VMEM((ZC, 2 * J, NZ), jnp.bfloat16),
            pltpu.SemaphoreType.DMA,
            pltpu.SemaphoreType.DMA((NY,)),
            pltpu.SemaphoreType.DMA,
            pltpu.SemaphoreType.DMA,
            pltpu.SemaphoreType.DMA,
            pltpu.SemaphoreType.DMA,
        ],
        compiler_params=pltpu.CompilerParams(
            collective_id=0, has_side_effects=True, vmem_limit_bytes=48 * 1024 * 1024
        ),
    )(
        focus,
        images,
        key,
        jnp.asarray(radius_table()),
        jnp.asarray(x_table()),
        jnp.asarray(tap_transform()),
        jnp.asarray(z_table()),
    )
    return out.transpose(1, 0, 2)[None]


def solution(mesh):
    placed = (
        P(("slab", "img"), None, None, None),
        P(("slab", "img")),
        P(("slab", "img")),
        P(("slab", "img")),
    )
    return jax.shard_map(
        on_device,
        mesh=mesh,
        in_specs=placed,
        out_specs=P("img", "slab", None, None),
        check_vma=False,
    )
```

profile of v0, /device:TPU:4, one launch (start us, length us, event | category | flops | bytes accessed | tf_op | source)
XLA Modules:
  0.0 59.1 jit_solution(8241352202502803458)
XLA Ops:
  0.0 0.0 copy-start.5
  0.0 0.7 %add_bitcast_fusion.key_ref = s32[1,128]{1,0:T(1,128)S(1)} fusion(s32[128]{0:T(128)} %param.9, s32[128]{0:T(128)} %param.10), kind=kLoop, calls=%fused_computation | loop fusion | flops 256 | bytes 1536 | tf_op jit(solution)/shard_map/reshape | solution.py:336
  0.7 0.0 copy-done.5
  0.7 0.0 copy-start
  0.7 1.2 %copy-done = bf16[128,2,4,512]{3,2,1,0:T(4,128)(2,1)S(1)} copy-done((bf16[128,2,4,512]{3,2,1,0:T(4,128)(2,1)S(1)}, bf16[128,2,4,512]{3,2,1,0:T(4,128)(2,1)}, u32[]{:S(2)}) %copy-start) | copy-done | bytes 1048600
  1.9 0.0 copy-start.1
  1.9 1.2 %copy-done.1 = bf16[512,1024]{1,0:T(8,128)(2,1)S(1)} copy-done((bf16[512,1024]{1,0:T(8,128)(2,1)S(1)}, bf16[512,1024]{1,0:T(8,128)(2,1)}, u32[]{:S(2)}) %copy-start.1) | copy-done | bytes 1048600
  3.1 0.0 copy-start.2
  3.2 1.2 %copy-done.2 = bf16[512,1024]{1,0:T(8,128)(2,1)S(1)} copy-done((bf16[512,1024]{1,0:T(8,128)(2,1)S(1)}, bf16[512,1024]{1,0:T(8,128)(2,1)}, u32[]{:S(2)}) %copy-start.2) | copy-done | bytes 1048600
  4.4 0.0 copy-start.3
  4.4 0.8 %copy-done.3 = bf16[2,8,1024]{2,1,0:T(8,128)(2,1)S(1)} copy-done((bf16[2,8,1024]{2,1,0:T(8,128)(2,1)S(1)}, bf16[2,8,1024]{2,1,0:T(8,128)(2,1)}, u32[]{:S(2)}) %copy-start.3) | copy-done | bytes 32792
  5.1 0.0 copy-start.4
  5.1 0.7 %copy-done.4 = f32[4,512]{1,0:T(4,128)S(1)} copy-done((f32[4,512]{1,0:T(4,128)S(1)}, f32[4,512]{1,0:T(4,128)}, u32[]{:S(2)}) %copy-start.4) | copy-done | bytes 8216
  5.8 52.7 %shard_map.82 = f32[2,8,512]{2,1,0:T(8,128)S(1)} custom-call(f32[128]{0:T(128)S(1)} %convert_multiply_fusion.focus_ref, bf16[128,2,4,512]{3,2,1,0:T(4,128)(2,1)S(1)} %copy-done, s32[1,128]{1,0:T(1,128)S(1)} %add_bitcast_fusion.key_ref, f32[4,512]{1,0:T(4,128)S(1)} %copy-done.4, bf16[512,1024]{1,0:T(8,128)(2,1)S(1)} %copy-done.2, ...), custom_call_target="tpu_custom_call" | custom-call | tf_op jit(solution)/shard_map/pallas_call | solution.py:339
  58.5 0.6 %copy.9 = f32[1,8,2,512]{3,2,1,0:T(2,128)} copy(f32[1,8,2,512]{3,1,2,0:T(8,128)S(1)} %bitcast.5) | data formatting | bytes 65536 | tf_op jit(solution)/shard_map/broadcast_in_dim | solution.py:373
  (1 shorter events, 0.0 us)
Async XLA Ops:
  0.0 0.7 %copy-start.5 = (bf16[128]{0:T(256)(128)(2,1)S(1)}, bf16[128]{0:T(256)(128)(2,1)}, u32[]{:S(2)}) copy-start(bf16[128]{0:T(256)(128)(2,1)} %param.11) | copy-start | bytes 772
  0.7 1.2 %copy-start = (bf16[128,2,4,512]{3,2,1,0:T(4,128)(2,1)S(1)}, bf16[128,2,4,512]{3,2,1,0:T(4,128)(2,1)}, u32[]{:S(2)}) copy-start(bf16[128,2,4,512]{3,2,1,0:T(4,128)(2,1)} %images_ref.1) | copy-start | bytes 3145732
  1.9 1.2 %copy-start.1 = (bf16[512,1024]{1,0:T(8,128)(2,1)S(1)}, bf16[512,1024]{1,0:T(8,128)(2,1)}, u32[]{:S(2)}) copy-start(bf16[512,1024]{1,0:T(8,128)(2,1)} %constant.15.clone.ztab_ref) | copy-start | bytes 3145732
  3.1 1.2 %copy-start.2 = (bf16[512,1024]{1,0:T(8,128)(2,1)S(1)}, bf16[512,1024]{1,0:T(8,128)(2,1)}, u32[]{:S(2)}) copy-start(bf16[512,1024]{1,0:T(8,128)(2,1)} %constant.13.clone.xtab_ref) | copy-start | bytes 3145732
  4.4 0.8 %copy-start.3 = (bf16[2,8,1024]{2,1,0:T(8,128)(2,1)S(1)}, bf16[2,8,1024]{2,1,0:T(8,128)(2,1)}, u32[]{:S(2)}) copy-start(bf16[2,8,1024]{2,1,0:T(8,128)(2,1)} %constant.14.clone.xtap_ref) | copy-start | bytes 98308
  5.1 0.7 %copy-start.4 = (f32[4,512]{1,0:T(4,128)S(1)}, f32[4,512]{1,0:T(4,128)}, u32[]{:S(2)}) copy-start(f32[4,512]{1,0:T(4,128)} %constant.12.clone.radius_ref) | copy-start | bytes 24580
where the time goes:
time: 59.5 us; the launch traced here: 59.1 us
  Pallas kernels  52.7 us (89%)
  local copies, waits for them, and re-layouts  5.77 us (10%)
  other arithmetic  0.69 us (1%)
    pallas_call x1, Pallas kernels, on_device(): pl.pallas_call(insertion_kernel, out_shape=jax.ShapeDtypeStruct((2, J, NZ...  52.7 us
    unnamed x12, local copies, waits for them, and re-layouts  5.13 us

commit v1 on v0

--- a/solution.py
+++ b/solution.py
@@ -25,6 +25,7 @@
 J = NX * CLASSES // (ZC * Q)
 K = NX // (Q * J)
 PLANE = NY * Q
+LOADS = 4
 
 MESH = pl.DeviceIdType.MESH
 
@@ -70,12 +71,6 @@
     return np.concatenate([high, low], axis=1)
 
 
-def radius_table():
-    signed = (np.arange(NX) + NX // 2) % NX - NX // 2
-    rows = np.arange(KY) + 1
-    return (rows[:, None] ** 2 + signed[None, :] ** 2).astype(np.float32)
-
-
 def sine_coefficients(terms):
     nodes = 0.25 + 0.25 * np.cos(np.pi * (np.arange(400) + 0.5) / 400)
     f = np.sqrt(nodes) * np.sqrt(0.5)
@@ -99,13 +94,16 @@
 
 def insertion_kernel(
     focus_ref,
+    key_ref,
+    images_hbm,
+    xtab_hbm,
+    xtap_hbm,
+    ztab_hbm,
+    out_ref,
     images_ref,
-    key_ref,
-    radius_ref,
     xtab_ref,
     xtap_ref,
     ztab_ref,
-    out_ref,
     rows_ref,
     factor_ref,
     send_ref,
@@ -121,6 +119,8 @@
     krecv_sem,
     zsend_sem,
     zrecv_sem,
+    image_sem,
+    table_sem,
 ):
     slab = lax.axis_index("slab")
     me_y = lax.axis_index("img")
@@ -150,10 +150,30 @@
             barrier, inc=1, device_id=z_peer(step), device_id_type=MESH
         )
 
-    radius = radius_ref[...]
-
-    @pl.loop(0, IMG_DEV, unroll=4)
-    def _(i):
+    per = IMG_DEV // LOADS
+    loads = [
+        pltpu.make_async_copy(
+            images_hbm.at[pl.ds(n * per, per)],
+            images_ref.at[pl.ds(n * per, per)],
+            image_sem.at[n],
+        )
+        for n in range(LOADS)
+    ]
+    tables = [
+        pltpu.make_async_copy(source, target, table_sem.at[n])
+        for n, (source, target) in enumerate(
+            [(xtap_hbm, xtap_ref), (xtab_hbm, xtab_ref), (ztab_hbm, ztab_ref)]
+        )
+    ]
+    for copy in loads + tables:
+        copy.start()
+
+    x = lax.broadcasted_iota(jnp.int32, (KY, NX), 1)
+    signed = ((x + NX // 2) & (NX - 1)) - NX // 2
+    y = lax.broadcasted_iota(jnp.int32, (KY, NX), 0) + 1
+    radius = (y * y + signed * signed).astype(jnp.float32)
+
+    def weigh(i):
         ctf = sine_turns(focus_ref[i] * radius + 0.1 / (2 * math.pi))
         value = jnp.concatenate(
             [ctf * images_ref[i, r].astype(jnp.float32) for r in range(2)], axis=0
@@ -163,6 +183,11 @@
                 :, b * 128 : (b + 1) * 128
             ]
 
+    for n in range(LOADS):
+        loads[n].wait()
+        pl.loop(n * per, (n + 1) * per, unroll=4)(weigh)
+
+    tables[0].wait()
     key = key_ref[...]
     xbin = jnp.broadcast_to(key & (XBINS - 1), (8, IMG_DEV))
     row = lax.broadcasted_iota(jnp.int32, (8, IMG_DEV), 0)
@@ -176,21 +201,7 @@
             chosen, xtap_ref[part], preferred_element_type=jnp.float32
         )
 
-    pl.semaphore_wait(barrier, PLANE - 1 + ZC - 1)
-
-    own_key = pltpu.make_async_copy(key_ref, keys_ref.at[0], krecv_sem)
-    own_key.start()
-
-    @pl.loop(1, PLANE)
-    def _(step):
-        pltpu.make_async_remote_copy(
-            src_ref=key_ref,
-            dst_ref=keys_ref.at[step],
-            send_sem=ksend_sem,
-            recv_sem=krecv_sem,
-            device_id=plane_peer(step // Q, lax.rem(step, Q)),
-            device_id_type=MESH,
-        ).start()
+    tables[1].wait()
 
     half = NX // K
 
@@ -240,8 +251,23 @@
             ).start()
 
     order = (2, 1, 3, 0)
-    for dy in order:
+    for n, dy in enumerate(order):
         transform(lax.rem(me_y + dy, NY))
+        if n == 0:
+            pl.semaphore_wait(barrier, PLANE - 1 + ZC - 1)
+            pltpu.make_async_copy(key_ref, keys_ref.at[0], krecv_sem).start()
+
+            @pl.loop(1, PLANE)
+            def _(step):
+                pltpu.make_async_remote_copy(
+                    src_ref=key_ref,
+                    dst_ref=keys_ref.at[step],
+                    send_sem=ksend_sem,
+                    recv_sem=krecv_sem,
+                    device_id=plane_peer(step // Q, lax.rem(step, Q)),
+                    device_id_type=MESH,
+                ).start()
+
         send_row(dy)
 
     pltpu.make_async_copy(keys_ref, keys_ref, krecv_sem).wait()
@@ -297,8 +323,10 @@
 
     pltpu.make_async_copy(zsend_ref.at[me_z], zrecv_ref.at[0], zrecv_sem).start()
 
-    @pl.loop(1, ZC)
-    def _(dz):
+    far_first = [ZC // 2]
+    for d in range(ZC // 2 - 1, 0, -1):
+        far_first += [d, ZC - d]
+    for dz in far_first:
         pltpu.make_async_remote_copy(
             src_ref=zsend_ref.at[lax.rem(me_z + dz, ZC)],
             dst_ref=zrecv_ref.at[dz],
@@ -308,6 +336,7 @@
             device_id_type=MESH,
         ).start()
 
+    tables[2].wait()
     pltpu.make_async_copy(zrecv_ref, zrecv_ref, zrecv_sem).wait()
 
     columns = jnp.zeros((2 * J, NZ), jnp.float32)
@@ -339,9 +368,14 @@
     out = pl.pallas_call(
         insertion_kernel,
         out_shape=jax.ShapeDtypeStruct((2, J, NZ), jnp.float32),
-        in_specs=[pl.BlockSpec(memory_space=pltpu.SMEM)] + [vmem] * 6,
+        in_specs=[pl.BlockSpec(memory_space=pltpu.SMEM), vmem]
+        + [pl.BlockSpec(memory_space=pl.ANY)] * 4,
         out_specs=vmem,
         scratch_shapes=[
+            pltpu.VMEM(images.shape, jnp.bfloat16),
+            pltpu.VMEM((NX, 2 * NX), jnp.bfloat16),
+            pltpu.VMEM((2, 8, 2 * NX), jnp.bfloat16),
+            pltpu.VMEM((NZ, 2 * NZ), jnp.bfloat16),
             pltpu.VMEM((NX // 128, IMG_DEV * 8, 128), jnp.float32),
             pltpu.VMEM((2, IMG_DEV, 2 * NX), jnp.float32),
             pltpu.VMEM((PLANE, IMG_DEV, 128), jnp.bfloat16),
@@ -357,15 +391,16 @@
             pltpu.SemaphoreType.DMA,
             pltpu.SemaphoreType.DMA,
             pltpu.SemaphoreType.DMA,
+            pltpu.SemaphoreType.DMA((LOADS,)),
+            pltpu.SemaphoreType.DMA((3,)),
         ],
         compiler_params=pltpu.CompilerParams(
-            collective_id=0, has_side_effects=True, vmem_limit_bytes=48 * 1024 * 1024
+            collective_id=0, has_side_effects=True, vmem_limit_bytes=60 * 1024 * 1024
         ),
     )(
         focus,
+        key,
         images,
-        key,
-        jnp.asarray(radius_table()),
         jnp.asarray(x_table()),
         jnp.asarray(tap_transform()),
         jnp.asarray(z_table()),

time: 59.5 us -> 53.8 us (0.904)
  the two profiles are of different devices: /device:TPU:4 before, /device:TPU:1 now
where the time goes in v1:
time: 53.8 us; the launch traced here: 53.2 us
  Pallas kernels  50 us (93%)
  other arithmetic  1.77 us (3%)
  local copies, waits for them, and re-layouts  1.4 us (3%)
    pallas_call x1, Pallas kernels, on_device(): pl.pallas_call(insertion_kernel, out_shape=jax.ShapeDtypeStruct((2, J, NZ...  50 us
    broadcast_in_dim x1, local copies, waits for them, and re-layouts, on_device(): return out.transpose(1, 0, 2)[None]  1.4 us
    reshape x1, other arithmetic, on_device(): key = (labels * (NZ * ZBINS * XBINS) + pose_bins).reshape(1, IMG_DEV)  1.26 us

profile of v1, /device:TPU:1, one launch (start us, length us, event | category | flops | bytes accessed | tf_op | source)
XLA Modules:
  0.0 53.2 jit_solution(14522355391330114031)
XLA Ops:
  0.0 0.0 copy-start
  0.0 1.3 %add_bitcast_fusion.key_ref = s32[1,128]{1,0:T(1,128)} fusion(s32[128]{0:T(128)} %param.8, s32[128]{0:T(128)} %param.9), kind=kLoop, calls=%fused_computation | loop fusion | flops 256 | bytes 1536 | tf_op jit(solution)/shard_map/reshape | solution.py:365
  1.3 0.0 copy-done
  1.3 0.5 convert_multiply_fusion.focus_ref
  1.8 50.0 %shard_map.73 = f32[2,8,512]{2,1,0:T(8,128)} custom-call(f32[128]{0:T(128)} %convert_multiply_fusion.focus_ref, s32[1,128]{1,0:T(1,128)} %add_bitcast_fusion.key_ref, bf16[128,2,4,512]{3,2,1,0:T(4,128)(2,1)} %images_hbm.1, bf16[512,1024]{1,0:T(8,128)(2,1)} %constant.10.clone.xtab_hbm, bf16[2,8,1024]{2,1,0:T(8,128)(2,1)} %constant.11.clone.xtap_hbm, ...), custom_call_target="tpu_custom_call" | custom-call | tf_op jit(solution)/shard_map/pallas_call | solution.py:368
  51.8 1.4 %copy.8 = f32[1,8,2,512]{3,2,1,0:T(2,128)} copy(f32[1,8,2,512]{3,1,2,0:T(8,128)} %bitcast.5) | data formatting | bytes 65536 | tf_op jit(solution)/shard_map/broadcast_in_dim | solution.py:408
Async XLA Ops:
  0.0 1.3 %copy-start = (bf16[128]{0:T(256)(128)(2,1)S(1)}, bf16[128]{0:T(256)(128)(2,1)}, u32[]{:S(2)}) copy-start(bf16[128]{0:T(256)(128)(2,1)} %param.10) | copy-start | bytes 772

commit v2 on v1

v2 whole, which is shorter than its diff:
```python
import math

import jax
import jax.numpy as jnp
import ml_dtypes
import numpy as np
from jax import lax
from jax.experimental import pallas as pl
from jax.experimental.pallas import tpu as pltpu
from jax.sharding import PartitionSpec as P

NX = 512
KY = 4
NZ = 512
CLASSES = 2
ZBINS = 4
XBINS = 4
TAPS = 8
IMG_DEV = 128
IMAGES = 65536

ZC = 16
Q = 8
NY = 4
J = NX * CLASSES // (ZC * Q)
K = NX // (Q * J)
PLANE = NY * Q
LOADS = 4
CHUNKS = 2
KC = K // CHUNKS
ROWS = KC * J

MESH = pl.DeviceIdType.MESH
BIG = pltpu.HBM


def tap_values(bins):
    fraction = (np.arange(bins) + 0.5) / bins
    distance = np.arange(TAPS)[None, :] - 3.0 - fraction[:, None]
    kernel = np.sinc(distance) * np.sinc(distance / 4.0)
    kernel = kernel / kernel.sum(axis=-1, keepdims=True)
    return kernel.astype(np.float32).astype(ml_dtypes.bfloat16).astype(np.float64)


def chunk_columns():
    n, q, k, j = np.meshgrid(
        np.arange(CHUNKS), np.arange(Q), np.arange(KC), np.arange(J), indexing="ij"
    )
    return (CHUNKS * k + n) * Q * J + q * J + j


def x_table():
    column = chunk_columns().reshape(CHUNKS, Q, 1, KC * J, 1)
    angle = 2 * np.pi / NX * ((column * np.arange(NX)) % NX)
    both = np.concatenate([np.cos(angle), np.sin(angle)], axis=2)
    return both.reshape(CHUNKS, Q * 2 * KC * J, NX).astype(ml_dtypes.bfloat16)


def z_table():
    index = np.arange(NZ)
    angle = 2 * np.pi / NZ * ((index[:, None] * index[None, :]) % NZ)
    return np.concatenate([np.cos(angle), np.sin(angle)], 1).astype(ml_dtypes.bfloat16)


def tap_transform():
    column = chunk_columns().reshape(-1)
    shift = np.arange(TAPS) - 3
    wave = np.exp(2j * np.pi / NX * ((column[:, None] * shift[None, :]) % NX))
    spectrum = wave @ tap_values(XBINS).T
    both = np.stack([spectrum.real, spectrum.imag])
    high = both.astype(np.float32).astype(ml_dtypes.bfloat16)
    low = (both - high.astype(np.float64)).astype(np.float32).astype(ml_dtypes.bfloat16)
    return np.concatenate([high, low], axis=2)


def sine_coefficients(terms):
    nodes = 0.25 + 0.25 * np.cos(np.pi * (np.arange(400) + 0.5) / 400)
    f = np.sqrt(nodes) * np.sqrt(0.5)
    basis = f[:, None] ** (2 * np.arange(terms)[None, :] + 1)
    scale = np.abs(basis).max(0)
    fit = np.linalg.lstsq(basis / scale, np.sin(2 * np.pi * f), rcond=None)[0]
    return [float(v) for v in fit / scale]


SINE = sine_coefficients(8)


def sine_turns(turns):
    f = turns - jnp.round(turns)
    t = f * f
    value = jnp.full_like(t, SINE[-1])
    for c in SINE[-2::-1]:
        value = value * t + c
    return value * f


def nt_dot(a, b):
    return lax.dot_general(
        a, b, (((1,), (1,)), ((), ())), preferred_element_type=jnp.float32
    )


def insertion_kernel(
    pose_ref,
    label_ref,
    focus_ref,
    images_hbm,
    xtab_hbm,
    xtap_hbm,
    ztab_hbm,
    out_ref,
    images_ref,
    xtab_ref,
    xtap_ref,
    ztab_ref,
    depth_ref,
    rows_ref,
    both_ref,
    factor_ref,
    send_ref,
    recv_ref,
    key_ref,
    keys_ref,
    spread_ref,
    zsend_ref,
    zrecv_ref,
    send_sem,
    recv_sem,
    ksend_sem,
    krecv_sem,
    zsend_sem,
    zrecv_sem,
    image_sem,
    table_sem,
):
    slab = lax.axis_index("slab")
    me_y = lax.axis_index("img")
    me_z = slab // Q
    me_q = lax.rem(slab, Q)

    def plane_peer(dy, dq):
        return me_z * Q + lax.rem(me_q + dq, Q), lax.rem(me_y + dy, NY)

    def z_peer(dz):
        return lax.rem(me_z + dz, ZC) * Q + me_q, me_y

    per = IMG_DEV // LOADS
    loads = [
        pltpu.make_async_copy(
            images_hbm.at[pl.ds(n * per, per)],
            images_ref.at[pl.ds(n * per, per)],
            image_sem.at[n],
        )
        for n in range(LOADS)
    ]
    tables = [
        pltpu.make_async_copy(source, target, table_sem.at[n])
        for n, (source, target) in enumerate(
            [(xtap_hbm, xtap_ref), (xtab_hbm, xtab_ref), (ztab_hbm, ztab_ref)]
        )
    ]
    for copy in loads + tables:
        copy.start()

    barrier = pltpu.get_barrier_semaphore()

    @pl.loop(1, ZC)
    def _(step):
        pl.semaphore_signal(
            barrier, inc=1, device_id=z_peer(step), device_id_type=MESH
        )

    @pl.loop(1, PLANE)
    def _(step):
        pl.semaphore_signal(
            barrier,
            inc=1,
            device_id=plane_peer(step // Q, lax.rem(step, Q)),
            device_id_type=MESH,
        )

    key = label_ref[...] * (NZ * ZBINS * XBINS) + pose_ref[...]
    key_ref[...] = key
    depth_ref[...] = jnp.broadcast_to(
        focus_ref[...].astype(jnp.float32) * (200.0 / (NX * NX)), (IMG_DEV, IMG_DEV)
    ).T
    x = lax.broadcasted_iota(jnp.int32, (KY, NX), 1)
    signed = ((x + NX // 2) & (NX - 1)) - NX // 2
    y = lax.broadcasted_iota(jnp.int32, (KY, NX), 0) + 1
    radius = (y * y + signed * signed).astype(jnp.float32)

    def weigh(i):
        depth = jnp.broadcast_to(depth_ref[pl.ds(i, 1), :], (KY, 128))
        depth = jnp.concatenate([depth] * (NX // 128), axis=1)
        ctf = sine_turns(depth * radius + 0.1 / (2 * math.pi))
        value = jnp.concatenate(
            [ctf * images_ref[i, r].astype(jnp.float32) for r in range(2)], axis=0
        )
        for b in range(NX // 128):
            rows_ref[b, pl.ds(pl.multiple_of(i * 8, 8), 8), :] = value[
                :, b * 128 : (b + 1) * 128
            ]

    for n in range(LOADS):
        loads[n].wait()
        pl.loop(n * per, (n + 1) * per, unroll=4)(weigh)

    tables[0].wait()
    row = lax.broadcasted_iota(jnp.int32, (8, IMG_DEV), 0)
    xbin = jnp.broadcast_to(key & (XBINS - 1), (8, IMG_DEV))
    chosen = jnp.where(xbin == (row & (XBINS - 1)), 1.0, 0.0).astype(jnp.bfloat16)
    for part in range(2):
        factor_ref[part] = jnp.dot(
            xtap_ref[part], chosen, preferred_element_type=jnp.float32
        )
    tables[1].wait()

    def gather(ky):
        for r in range(2):
            for b in range(NX // 128):
                both_ref[
                    ky, r * IMG_DEV : (r + 1) * IMG_DEV, b * 128 : (b + 1) * 128
                ] = rows_ref[b, pl.ds(r * KY + ky, IMG_DEV, stride=8), :].astype(
                    jnp.bfloat16
                )

    def transform(chunk, ky):
        product = nt_dot(xtab_ref[chunk], both_ref[ky])
        for q in range(Q):
            top = q * 2 * ROWS
            cosine = product[top : top + ROWS]
            sine = product[top + ROWS : top + 2 * ROWS]
            real = cosine[:, :IMG_DEV] - sine[:, IMG_DEV:]
            imag = sine[:, :IMG_DEV] + cosine[:, IMG_DEV:]
            at = slice((chunk * Q + q) * ROWS, (chunk * Q + q + 1) * ROWS)
            tap_real, tap_imag = factor_ref[0, at], factor_ref[1, at]
            send_ref[chunk, ky * Q + q] = jnp.concatenate(
                [
                    real * tap_real - imag * tap_imag,
                    real * tap_imag + imag * tap_real,
                ],
                axis=0,
            ).astype(jnp.bfloat16)

    def send_row(chunk, dy):
        ky = lax.rem(me_y + dy, NY)
        if dy == 0:
            pltpu.make_async_copy(
                send_ref.at[chunk, ky * Q + me_q],
                recv_ref.at[chunk, 0],
                recv_sem.at[chunk, 0],
            ).start()

        @pl.loop(1 if dy == 0 else 0, Q)
        def _(dq):
            pltpu.make_async_remote_copy(
                src_ref=send_ref.at[chunk, ky * Q + lax.rem(me_q + dq, Q)],
                dst_ref=recv_ref.at[chunk, dy * Q + dq],
                send_sem=send_sem.at[chunk],
                recv_sem=recv_sem.at[chunk, dy],
                device_id=plane_peer(dy, dq),
                device_id_type=MESH,
            ).start()

    order = (2, 1, 3, 0)
    for chunk in range(CHUNKS):
        for n, dy in enumerate(order):
            ky = lax.rem(me_y + dy, NY)
            if chunk == 0:
                gather(ky)
            transform(chunk, ky)
            if chunk == 0 and n == 0:
                pl.semaphore_wait(barrier, PLANE - 1 + ZC - 1)
                pltpu.make_async_copy(key_ref, keys_ref.at[0], krecv_sem).start()

                @pl.loop(1, PLANE)
                def _(step):
                    pltpu.make_async_remote_copy(
                        src_ref=key_ref,
                        dst_ref=keys_ref.at[step],
                        send_sem=ksend_sem,
                        recv_sem=krecv_sem,
                        device_id=plane_peer(step // Q, lax.rem(step, Q)),
                        device_id_type=MESH,
                    ).start()

            send_row(chunk, dy)

    pltpu.make_async_copy(keys_ref, keys_ref, krecv_sem).wait()
    ztaps = tap_values(ZBINS)
    sub = lax.broadcasted_iota(jnp.int32, (16, IMG_DEV), 0)

    @pl.loop(0, PLANE)
    def _(slot):
        entry = keys_ref[slot]
        zbin = (entry >> 2) & (ZBINS - 1)
        start = (entry >> 4) & (NZ - 1)
        label = entry >> 13
        low = jnp.broadcast_to(start & 15, (16, IMG_DEV))
        offset = (sub - low) & 15
        base = jnp.broadcast_to(start >> 4, (16, IMG_DEV))
        base = (base + jnp.where(sub < low, 1, 0)) & 31
        block = base + jnp.broadcast_to(label * 32, (16, IMG_DEV))
        pattern = jnp.zeros((16, IMG_DEV), jnp.float32)
        for t in range(TAPS):
            tap = jnp.full((1, IMG_DEV), float(ztaps[0, t]), jnp.float32)
            for b in range(1, ZBINS):
                tap = jnp.where(zbin == b, float(ztaps[b, t]), tap)
            pattern = jnp.where(
                offset == t, jnp.broadcast_to(tap, (16, IMG_DEV)), pattern
            )
        lanes = pl.ds(pl.multiple_of(lax.rem(slot, Q) * IMG_DEV, IMG_DEV), IMG_DEV)
        for b in range(CLASSES * NZ // 16):
            spread_ref[slot // Q, b * 16 : (b + 1) * 16, lanes] = jnp.where(
                block == b, pattern, 0.0
            ).astype(jnp.bfloat16)

    odd = lax.rem(me_z, 2)
    for chunk in range(CHUNKS):
        volume = None
        for dy in order:
            arrived = recv_ref.at[chunk, pl.ds(dy * Q, Q)]
            pltpu.make_async_copy(arrived, arrived, recv_sem.at[chunk, dy]).wait()
            part = nt_dot(
                jnp.concatenate(
                    [recv_ref[chunk, dy * Q + q] for q in range(Q)], axis=1
                ),
                spread_ref[dy],
            )
            volume = part if volume is None else volume + part
        for c in range(CLASSES):
            planes = slice(c * NZ, (c + 1) * NZ)
            for k in range(KC):
                zsend_ref[c * K + k * CHUNKS + chunk] = jnp.concatenate(
                    [
                        volume[r * ROWS + k * J : r * ROWS + (k + 1) * J, planes]
                        for r in range(2)
                    ],
                    axis=0,
                ).astype(jnp.bfloat16)

        apart = lax.rem(odd + chunk, 2)

        def to_z(dz):
            pltpu.make_async_remote_copy(
                src_ref=zsend_ref.at[lax.rem(me_z + dz, ZC)],
                dst_ref=zrecv_ref.at[dz],
                send_sem=zsend_sem,
                recv_sem=zrecv_sem,
                device_id=z_peer(dz),
                device_id_type=MESH,
            ).start()

        same = [8, 6, 10, 4, 12, 2, 14]
        other = [7, 9, 5, 11, 3, 13, 1]
        for a, b in zip(same, other):
            to_z(a + apart * (b - a))

        @pl.when(apart == 1)
        def _():
            to_z(ZC - 1)

        @pl.when(apart == 0)
        def _():
            pltpu.make_async_copy(
                zsend_ref.at[me_z], zrecv_ref.at[0], zrecv_sem
            ).start()

    tables[2].wait()
    pltpu.make_async_copy(zrecv_ref, zrecv_ref, zrecv_sem).wait()

    columns = jnp.zeros((2 * J, NZ), jnp.float32)
    for dz in range(ZC):
        columns = columns + zrecv_ref[dz].astype(jnp.float32)
    high = columns.astype(jnp.bfloat16)
    low = (columns - high.astype(jnp.float32)).astype(jnp.bfloat16)
    waves = jnp.dot(
        jnp.concatenate([high, low], axis=0),
        ztab_ref[...],
        preferred_element_type=jnp.float32,
    )
    waves = (waves[: 2 * J] + waves[2 * J :]) * (2.5 / math.sqrt(IMAGES * NX))
    out_ref[0] = waves[:J, :NZ] - waves[J:, NZ:]
    out_ref[1] = waves[:J, NZ:] + waves[J:, :NZ]

    for chunk in range(CHUNKS):
        plane_sent = send_ref.at[chunk, pl.ds(0, PLANE - 1)]
        pltpu.make_async_copy(plane_sent, plane_sent, send_sem.at[chunk]).wait()
    keys_sent = keys_ref.at[pl.ds(0, PLANE - 1)]
    pltpu.make_async_copy(keys_sent, keys_sent, ksend_sem).wait()
    z_sent = zsend_ref.at[pl.ds(0, ZC - 1)]
    pltpu.make_async_copy(z_sent, z_sent, zsend_sem).wait()


def on_device(images, pose_bins, labels, defocus):
    vmem = pl.BlockSpec(memory_space=pltpu.VMEM)
    out = pl.pallas_call(
        insertion_kernel,
        out_shape=jax.ShapeDtypeStruct((2, J, NZ), jnp.float32),
        in_specs=[vmem] * 3 + [pl.BlockSpec(memory_space=BIG)] * 4,
        out_specs=vmem,
        scratch_shapes=[
            pltpu.VMEM(images.shape, jnp.bfloat16),
            pltpu.VMEM((CHUNKS, NX, NX), jnp.bfloat16),
            pltpu.VMEM((2, NX, 8), jnp.bfloat16),
            pltpu.VMEM((NZ, 2 * NZ), jnp.bfloat16),
            pltpu.VMEM((IMG_DEV, IMG_DEV), jnp.float32),
            pltpu.VMEM((NX // 128, IMG_DEV * 8, 128), jnp.float32),
            pltpu.VMEM((KY, 2 * IMG_DEV, NX), jnp.bfloat16),
            pltpu.VMEM((2, NX, IMG_DEV), jnp.float32),
            pltpu.VMEM((CHUNKS, PLANE, 2 * ROWS, IMG_DEV), jnp.bfloat16),
            pltpu.VMEM((CHUNKS, PLANE, 2 * ROWS, IMG_DEV), jnp.bfloat16),
            pltpu.VMEM((1, IMG_DEV), jnp.int32),
            pltpu.VMEM((PLANE, 1, IMG_DEV), jnp.int32),
            pltpu.VMEM((NY, CLASSES * NZ, Q * IMG_DEV), jnp.bfloat16),
            pltpu.VMEM((ZC, 2 * J, NZ), jnp.bfloat16),
            pltpu.VMEM((ZC, 2 * J, NZ), jnp.bfloat16),
            pltpu.SemaphoreType.DMA((CHUNKS,)),
            pltpu.SemaphoreType.DMA((CHUNKS, NY)),
            pltpu.SemaphoreType.DMA,
            pltpu.SemaphoreType.DMA,
            pltpu.SemaphoreType.DMA,
            pltpu.SemaphoreType.DMA,
            pltpu.SemaphoreType.DMA((LOADS,)),
            pltpu.SemaphoreType.DMA((3,)),
        ],
        compiler_params=pltpu.CompilerParams(
            collective_id=0, has_side_effects=True, vmem_limit_bytes=55040 * 1024
        ),
    )(
        pose_bins.reshape(1, IMG_DEV),
        labels.reshape(1, IMG_DEV),
        defocus.reshape(1, IMG_DEV),
        images,
        jnp.asarray(x_table()),
        jnp.asarray(tap_transform()),
        jnp.asarray(z_table()),
    )
    return out.transpose(1, 0, 2)[None]


def solution(mesh):
    placed = (
        P(("slab", "img"), None, None, None),
        P(("slab", "img")),
        P(("slab", "img")),
        P(("slab", "img")),
    )
    return jax.shard_map(
        on_device,
        mesh=mesh,
        in_specs=placed,
        out_specs=P("img", "slab", None, None),
        check_vma=False,
    )
```

time: 53.8 us -> 47.3 us (0.88)
  the two profiles are of different devices: /device:TPU:1 before, /device:TPU:38 now
where the time goes in v2:
time: 47.3 us; the launch traced here: 47.2 us
  Pallas kernels  45.9 us (97%)
  local copies, waits for them, and re-layouts  1.32 us (3%)
    pallas_call x1, Pallas kernels, on_device(): pl.pallas_call(insertion_kernel, out_shape=jax.ShapeDtypeStruct((2, J, NZ...  45.9 us

profile of v2, /device:TPU:38, one launch (start us, length us, event | category | flops | bytes accessed | tf_op | source)
XLA Modules:
  0.0 47.2 jit_solution(5824194795912433615)
XLA Ops:
  0.0 0.0 copy-start
  0.0 0.0 copy-start.1
  0.0 0.0 copy-start.2
  0.0 0.6 %copy-done = s32[128]{0:T(128)S(1)} copy-done((s32[128]{0:T(128)S(1)}, s32[128]{0:T(128)}, u32[]{:S(2)}) %copy-start) | copy-done | bytes 536
  0.7 0.0 copy-done.1
  0.7 0.0 copy-done.2
  0.7 45.9 %shard_map.73 = f32[2,8,512]{2,1,0:T(8,128)S(1)} custom-call(s32[1,128]{1,0:T(1,128)S(1)} %bitcast.7, s32[1,128]{1,0:T(1,128)S(1)} %bitcast.8, bf16[1,128]{1,0:T(2,128)(2,1)S(1)} %bitcast.9, bf16[128,2,4,512]{3,2,1,0:T(4,128)(2,1)} %images_hbm.1, bf16[2,512,512]{2,1,0:T(8,128)(2,1)} %constant.6.clone.xtab_hbm, bf16[2,512,8]{2,1,0:T(8,128)(2,1)} %constant.7.clone.xtap_hbm, ...), custom_call_target="tpu_custom_call" | custom-call | tf_op jit(solution)/shard_map/pallas_call | solution.py:397
  46.6 0.6 %copy.8 = f32[1,8,2,512]{3,2,1,0:T(2,128)} copy(f32[1,8,2,512]{3,1,2,0:T(8,128)S(1)} %bitcast.6) | data formatting | bytes 65536 | tf_op jit(solution)/shard_map/broadcast_in_dim | solution.py:439
Async XLA Ops:
  0.0 0.7 %copy-start = (s32[128]{0:T(128)S(1)}, s32[128]{0:T(128)}, u32[]{:S(2)}) copy-start(s32[128]{0:T(128)} %param.8) | copy-start | bytes 1540
  0.0 0.7 %copy-start.1 = (s32[128]{0:T(128)S(1)}, s32[128]{0:T(128)}, u32[]{:S(2)}) copy-start(s32[128]{0:T(128)} %param.9) | copy-start | bytes 1540
  0.0 0.7 %copy-start.2 = (bf16[128]{0:T(256)(128)(2,1)S(1)}, bf16[128]{0:T(256)(128)(2,1)}, u32[]{:S(2)}) copy-start(bf16[128]{0:T(256)(128)(2,1)} %param.10) | copy-start | bytes 772

commit v3 on v2

--- a/solution.py
+++ b/solution.py
@@ -26,9 +26,12 @@
 K = NX // (Q * J)
 PLANE = NY * Q
 LOADS = 4
-CHUNKS = 2
+CHUNKS = 4
 KC = K // CHUNKS
 ROWS = KC * J
+FAR_FIRST = sorted(range(1, ZC // CHUNKS), key=lambda n: abs(n * CHUNKS - ZC // 2))
+ACROSS = [(dx, flip) for dx in (2, 1, 3, 0) for flip in (0, 1)]
+ROW_GROUPS = ((2,), (1, 3), (0,))
 
 MESH = pl.DeviceIdType.MESH
 BIG = pltpu.HBM
@@ -82,7 +85,7 @@
     return [float(v) for v in fit / scale]
 
 
-SINE = sine_coefficients(8)
+SINE = sine_coefficients(7)
 
 
 def sine_turns(turns):
@@ -137,9 +140,25 @@
     me_y = lax.axis_index("img")
     me_z = slab // Q
     me_q = lax.rem(slab, Q)
-
-    def plane_peer(dy, dq):
-        return me_z * Q + lax.rem(me_q + dq, Q), lax.rem(me_y + dy, NY)
+    me_x, me_core = me_q // 2, lax.rem(me_q, 2)
+    peer_q = {
+        (dx, flip): lax.rem(me_x + dx, Q // 2) * 2 + lax.rem(me_core + flip, 2)
+        for dx, flip in ACROSS
+    }
+    peer_y = [lax.rem(me_y + dy, NY) for dy in range(NY)]
+    partners = [
+        (dy, across)
+        for group in ROW_GROUPS
+        for across in ACROSS
+        for dy in group
+        if (dy, across) != (0, (0, 0))
+    ]
+
+    def plane_peer(dy, across):
+        return me_z * Q + peer_q[across], peer_y[dy]
+
+    def slot_of(dy, across):
+        return dy * Q + across[0] * 2 + across[1]
 
     def z_peer(dz):
         return lax.rem(me_z + dz, ZC) * Q + me_q, me_y
@@ -170,13 +189,9 @@
             barrier, inc=1, device_id=z_peer(step), device_id_type=MESH
         )
 
-    @pl.loop(1, PLANE)
-    def _(step):
+    for partner in partners:
         pl.semaphore_signal(
-            barrier,
-            inc=1,
-            device_id=plane_peer(step // Q, lax.rem(step, Q)),
-            device_id_type=MESH,
+            barrier, inc=1, device_id=plane_peer(*partner), device_id_type=MESH
         )
 
     key = label_ref[...] * (NZ * ZBINS * XBINS) + pose_ref[...]
@@ -184,17 +199,10 @@
     depth_ref[...] = jnp.broadcast_to(
         focus_ref[...].astype(jnp.float32) * (200.0 / (NX * NX)), (IMG_DEV, IMG_DEV)
     ).T
-    x = lax.broadcasted_iota(jnp.int32, (KY, NX), 1)
-    signed = ((x + NX // 2) & (NX - 1)) - NX // 2
-    y = lax.broadcasted_iota(jnp.int32, (KY, NX), 0) + 1
-    radius = (y * y + signed * signed).astype(jnp.float32)
-
-    def weigh(i):
-        depth = jnp.broadcast_to(depth_ref[pl.ds(i, 1), :], (KY, 128))
-        depth = jnp.concatenate([depth] * (NX // 128), axis=1)
-        ctf = sine_turns(depth * radius + 0.1 / (2 * math.pi))
+
+    def unpack(i):
         value = jnp.concatenate(
-            [ctf * images_ref[i, r].astype(jnp.float32) for r in range(2)], axis=0
+            [images_ref[i, r].astype(jnp.float32) for r in range(2)], axis=0
         )
         for b in range(NX // 128):
             rows_ref[b, pl.ds(pl.multiple_of(i * 8, 8), 8), :] = value[
@@ -203,7 +211,7 @@
 
     for n in range(LOADS):
         loads[n].wait()
-        pl.loop(n * per, (n + 1) * per, unroll=4)(weigh)
+        pl.loop(n * per, (n + 1) * per, unroll=8)(unpack)
 
     tables[0].wait()
     row = lax.broadcasted_iota(jnp.int32, (8, IMG_DEV), 0)
@@ -215,14 +223,20 @@
         )
     tables[1].wait()
 
-    def gather(ky):
-        for r in range(2):
-            for b in range(NX // 128):
+    lane = lax.broadcasted_iota(jnp.int32, (1, 128), 1)
+
+    def weigh(ky):
+        for b in range(NX // 128):
+            signed = (
+                ((lane + (b * 128 + NX // 2)) & (NX - 1)) - NX // 2
+            )
+            radius = (signed * signed + (ky + 1) * (ky + 1)).astype(jnp.float32)
+            ctf = sine_turns(depth_ref[...] * radius + 0.1 / (2 * math.pi))
+            for r in range(2):
+                image = rows_ref[b, pl.ds(r * KY + ky, IMG_DEV, stride=8), :]
                 both_ref[
                     ky, r * IMG_DEV : (r + 1) * IMG_DEV, b * 128 : (b + 1) * 128
-                ] = rows_ref[b, pl.ds(r * KY + ky, IMG_DEV, stride=8), :].astype(
-                    jnp.bfloat16
-                )
+                ] = (ctf * image).astype(jnp.bfloat16)
 
     def transform(chunk, ky):
         product = nt_dot(xtab_ref[chunk], both_ref[ky])
@@ -242,49 +256,47 @@
                 axis=0,
             ).astype(jnp.bfloat16)
 
-    def send_row(chunk, dy):
-        ky = lax.rem(me_y + dy, NY)
-        if dy == 0:
+    def send(chunk, dy, across):
+        slot = slot_of(dy, across)
+        block = send_ref.at[chunk, peer_y[dy] * Q + peer_q[across]]
+        if slot == 0:
             pltpu.make_async_copy(
-                send_ref.at[chunk, ky * Q + me_q],
-                recv_ref.at[chunk, 0],
-                recv_sem.at[chunk, 0],
+                block, recv_ref.at[chunk, 0], recv_sem.at[chunk, 0]
             ).start()
-
-        @pl.loop(1 if dy == 0 else 0, Q)
-        def _(dq):
+        else:
             pltpu.make_async_remote_copy(
-                src_ref=send_ref.at[chunk, ky * Q + lax.rem(me_q + dq, Q)],
-                dst_ref=recv_ref.at[chunk, dy * Q + dq],
+                src_ref=block,
+                dst_ref=recv_ref.at[chunk, slot],
                 send_sem=send_sem.at[chunk],
                 recv_sem=recv_sem.at[chunk, dy],
-                device_id=plane_peer(dy, dq),
+                device_id=plane_peer(dy, across),
                 device_id_type=MESH,
             ).start()
 
-    order = (2, 1, 3, 0)
+    def send_keys():
+        pltpu.make_async_copy(key_ref, keys_ref.at[0], krecv_sem).start()
+        for partner in partners:
+            pltpu.make_async_remote_copy(
+                src_ref=key_ref,
+                dst_ref=keys_ref.at[slot_of(*partner)],
+                send_sem=ksend_sem,
+                recv_sem=krecv_sem,
+                device_id=plane_peer(*partner),
+                device_id_type=MESH,
+            ).start()
+
     for chunk in range(CHUNKS):
-        for n, dy in enumerate(order):
-            ky = lax.rem(me_y + dy, NY)
-            if chunk == 0:
-                gather(ky)
-            transform(chunk, ky)
-            if chunk == 0 and n == 0:
+        for group in ROW_GROUPS:
+            for dy in group:
+                if chunk == 0:
+                    weigh(peer_y[dy])
+                transform(chunk, peer_y[dy])
+            if chunk == 0 and group == ROW_GROUPS[0]:
                 pl.semaphore_wait(barrier, PLANE - 1 + ZC - 1)
-                pltpu.make_async_copy(key_ref, keys_ref.at[0], krecv_sem).start()
-
-                @pl.loop(1, PLANE)
-                def _(step):
-                    pltpu.make_async_remote_copy(
-                        src_ref=key_ref,
-                        dst_ref=keys_ref.at[step],
-                        send_sem=ksend_sem,
-                        recv_sem=krecv_sem,
-                        device_id=plane_peer(step // Q, lax.rem(step, Q)),
-                        device_id_type=MESH,
-                    ).start()
-
-            send_row(chunk, dy)
+                send_keys()
+            for across in ACROSS:
+                for dy in group:
+                    send(chunk, dy, across)
 
     pltpu.make_async_copy(keys_ref, keys_ref, krecv_sem).wait()
     ztaps = tap_values(ZBINS)
@@ -315,10 +327,9 @@
                 block == b, pattern, 0.0
             ).astype(jnp.bfloat16)
 
-    odd = lax.rem(me_z, 2)
     for chunk in range(CHUNKS):
         volume = None
-        for dy in order:
+        for dy in (dy for group in ROW_GROUPS for dy in group):
             arrived = recv_ref.at[chunk, pl.ds(dy * Q, Q)]
             pltpu.make_async_copy(arrived, arrived, recv_sem.at[chunk, dy]).wait()
             part = nt_dot(
@@ -339,7 +350,7 @@
                     axis=0,
                 ).astype(jnp.bfloat16)
 
-        apart = lax.rem(odd + chunk, 2)
+        apart = lax.rem(me_z * (CHUNKS - 1) + chunk, CHUNKS)
 
         def to_z(dz):
             pltpu.make_async_remote_copy(
@@ -351,14 +362,12 @@
                 device_id_type=MESH,
             ).start()
 
-        same = [8, 6, 10, 4, 12, 2, 14]
-        other = [7, 9, 5, 11, 3, 13, 1]
-        for a, b in zip(same, other):
-            to_z(a + apart * (b - a))
-
-        @pl.when(apart == 1)
+        for far in FAR_FIRST:
+            to_z(apart + far * CHUNKS)
+
+        @pl.when(apart != 0)
         def _():
-            to_z(ZC - 1)
+            to_z(apart)
 
         @pl.when(apart == 0)
         def _():
@@ -401,7 +410,7 @@
         out_specs=vmem,
         scratch_shapes=[
             pltpu.VMEM(images.shape, jnp.bfloat16),
-            pltpu.VMEM((CHUNKS, NX, NX), jnp.bfloat16),
+            pltpu.VMEM((CHUNKS, 2 * NX // CHUNKS, NX), jnp.bfloat16),
             pltpu.VMEM((2, NX, 8), jnp.bfloat16),
             pltpu.VMEM((NZ, 2 * NZ), jnp.bfloat16),
             pltpu.VMEM((IMG_DEV, IMG_DEV), jnp.float32),

time: 47.3 us -> 43.1 us (0.911)
  the two profiles are of different devices: /device:TPU:38 before, /device:TPU:1 now
where the time goes in v3:
time: 43.1 us; the launch traced here: 42.4 us
  Pallas kernels  41 us (95%)
  local copies, waits for them, and re-layouts  1.32 us (3%)
    pallas_call x1, Pallas kernels, on_device(): pl.pallas_call(insertion_kernel, out_shape=jax.ShapeDtypeStruct((2, J, NZ...  41 us

profile of v3, /device:TPU:1, one launch (start us, length us, event | category | flops | bytes accessed | tf_op | source)
XLA Modules:
  0.0 42.4 jit_solution(16920363645495154662)
XLA Ops:
  0.0 0.0 copy-start
  0.0 0.0 copy-start.1
  0.0 0.0 copy-start.2
  0.0 0.6 %copy-done = s32[128]{0:T(128)S(1)} copy-done((s32[128]{0:T(128)S(1)}, s32[128]{0:T(128)}, u32[]{:S(2)}) %copy-start) | copy-done | bytes 536
  0.7 0.0 copy-done.1
  0.7 0.0 copy-done.2
  0.7 41.0 %shard_map.73 = f32[2,8,512]{2,1,0:T(8,128)S(1)} custom-call(s32[1,128]{1,0:T(1,128)S(1)} %bitcast.7, s32[1,128]{1,0:T(1,128)S(1)} %bitcast.8, bf16[1,128]{1,0:T(2,128)(2,1)S(1)} %bitcast.9, bf16[128,2,4,512]{3,2,1,0:T(4,128)(2,1)} %images_hbm.1, bf16[4,256,512]{2,1,0:T(8,128)(2,1)} %constant.6.clone.xtab_hbm, bf16[2,512,8]{2,1,0:T(8,128)(2,1)} %constant.7.clone.xtap_hbm, ...), custom_call_target="tpu_custom_call" | custom-call | tf_op jit(solution)/shard_map/pallas_call | solution.py:406
  41.7 0.6 %copy.8 = f32[1,8,2,512]{3,2,1,0:T(2,128)} copy(f32[1,8,2,512]{3,1,2,0:T(8,128)S(1)} %bitcast.6) | data formatting | bytes 65536 | tf_op jit(solution)/shard_map/broadcast_in_dim | solution.py:448
Async XLA Ops:
  0.0 0.7 %copy-start = (s32[128]{0:T(128)S(1)}, s32[128]{0:T(128)}, u32[]{:S(2)}) copy-start(s32[128]{0:T(128)} %param.8) | copy-start | bytes 1540
  0.0 0.7 %copy-start.1 = (s32[128]{0:T(128)S(1)}, s32[128]{0:T(128)}, u32[]{:S(2)}) copy-start(s32[128]{0:T(128)} %param.9) | copy-start | bytes 1540
  0.0 0.7 %copy-start.2 = (bf16[128]{0:T(256)(128)(2,1)S(1)}, bf16[128]{0:T(256)(128)(2,1)}, u32[]{:S(2)}) copy-start(bf16[128]{0:T(256)(128)(2,1)} %param.10) | copy-start | bytes 772

commit v4 on v3

--- a/solution.py
+++ b/solution.py
@@ -29,7 +29,7 @@
 CHUNKS = 4
 KC = K // CHUNKS
 ROWS = KC * J
-FAR_FIRST = sorted(range(1, ZC // CHUNKS), key=lambda n: abs(n * CHUNKS - ZC // 2))
+TOGETHER = ((0,), (1,), (2,), (3,))
 ACROSS = [(dx, flip) for dx in (2, 1, 3, 0) for flip in (0, 1)]
 ROW_GROUPS = ((2,), (1, 3), (0,))
 
@@ -49,7 +49,7 @@
     n, q, k, j = np.meshgrid(
         np.arange(CHUNKS), np.arange(Q), np.arange(KC), np.arange(J), indexing="ij"
     )
-    return (CHUNKS * k + n) * Q * J + q * J + j
+    return (KC * n + k) * Q * J + q * J + j
 
 
 def x_table():
@@ -135,6 +135,7 @@
     zrecv_sem,
     image_sem,
     table_sem,
+    greet_sem,
 ):
     slab = lax.axis_index("slab")
     me_y = lax.axis_index("img")
@@ -183,11 +184,19 @@
 
     barrier = pltpu.get_barrier_semaphore()
 
-    @pl.loop(1, ZC)
-    def _(step):
+    for dz in (1, ZC - 1):
         pl.semaphore_signal(
-            barrier, inc=1, device_id=z_peer(step), device_id_type=MESH
-        )
+            barrier, inc=1, device_id=z_peer(dz), device_id_type=MESH
+        )
+
+    def greet(n):
+        for dz in (2**n, ZC - 2**n):
+            pl.semaphore_signal(
+                greet_sem.at[n], inc=1, device_id=z_peer(dz), device_id_type=MESH
+            )
+
+    def greeted(n):
+        pl.semaphore_wait(greet_sem.at[n], 2)
 
     for partner in partners:
         pl.semaphore_signal(
@@ -292,18 +301,21 @@
                     weigh(peer_y[dy])
                 transform(chunk, peer_y[dy])
             if chunk == 0 and group == ROW_GROUPS[0]:
-                pl.semaphore_wait(barrier, PLANE - 1 + ZC - 1)
+                pl.semaphore_wait(barrier, PLANE - 1 + 2)
+                greet(0)
                 send_keys()
             for across in ACROSS:
                 for dy in group:
                     send(chunk, dy, across)
 
+    greeted(0)
+    greet(1)
+
     pltpu.make_async_copy(keys_ref, keys_ref, krecv_sem).wait()
     ztaps = tap_values(ZBINS)
     sub = lax.broadcasted_iota(jnp.int32, (16, IMG_DEV), 0)
 
-    @pl.loop(0, PLANE)
-    def _(slot):
+    def spread(slot):
         entry = keys_ref[slot]
         zbin = (entry >> 2) & (ZBINS - 1)
         start = (entry >> 4) & (NZ - 1)
@@ -322,35 +334,29 @@
                 offset == t, jnp.broadcast_to(tap, (16, IMG_DEV)), pattern
             )
         lanes = pl.ds(pl.multiple_of(lax.rem(slot, Q) * IMG_DEV, IMG_DEV), IMG_DEV)
+        block = block.astype(jnp.float32).astype(jnp.bfloat16)
+        pattern = pattern.astype(jnp.bfloat16)
         for b in range(CLASSES * NZ // 16):
             spread_ref[slot // Q, b * 16 : (b + 1) * 16, lanes] = jnp.where(
-                block == b, pattern, 0.0
-            ).astype(jnp.bfloat16)
-
-    for chunk in range(CHUNKS):
-        volume = None
-        for dy in (dy for group in ROW_GROUPS for dy in group):
-            arrived = recv_ref.at[chunk, pl.ds(dy * Q, Q)]
-            pltpu.make_async_copy(arrived, arrived, recv_sem.at[chunk, dy]).wait()
-            part = nt_dot(
-                jnp.concatenate(
-                    [recv_ref[chunk, dy * Q + q] for q in range(Q)], axis=1
-                ),
-                spread_ref[dy],
+                block == jnp.bfloat16(b), pattern, jnp.bfloat16(0)
             )
-            volume = part if volume is None else volume + part
+
+    pl.loop(0, PLANE // 2)(spread)
+    greeted(1)
+    greet(2)
+    pl.loop(PLANE // 2, PLANE)(spread)
+
+    def to_owners(chunk, volume):
         for c in range(CLASSES):
             planes = slice(c * NZ, (c + 1) * NZ)
             for k in range(KC):
-                zsend_ref[c * K + k * CHUNKS + chunk] = jnp.concatenate(
+                zsend_ref[c * K + chunk * KC + k] = jnp.concatenate(
                     [
                         volume[r * ROWS + k * J : r * ROWS + (k + 1) * J, planes]
                         for r in range(2)
                     ],
                     axis=0,
                 ).astype(jnp.bfloat16)
-
-        apart = lax.rem(me_z * (CHUNKS - 1) + chunk, CHUNKS)
 
         def to_z(dz):
             pltpu.make_async_remote_copy(
@@ -362,18 +368,44 @@
                 device_id_type=MESH,
             ).start()
 
-        for far in FAR_FIRST:
-            to_z(apart + far * CHUNKS)
-
-        @pl.when(apart != 0)
-        def _():
-            to_z(apart)
-
-        @pl.when(apart == 0)
-        def _():
-            pltpu.make_async_copy(
-                zsend_ref.at[me_z], zrecv_ref.at[0], zrecv_sem
-            ).start()
+        away = [lax.rem(chunk * KC + k + ZC - me_z, K) for k in range(KC)]
+        for dz in away:
+            to_z(dz + K)
+        for dz in away:
+
+            @pl.when(dz != 0)
+            def _():
+                to_z(dz)
+
+            @pl.when(dz == 0)
+            def _():
+                pltpu.make_async_copy(
+                    zsend_ref.at[me_z], zrecv_ref.at[0], zrecv_sem
+                ).start()
+
+    for together in TOGETHER:
+        volume = None
+        for dy in (dy for group in ROW_GROUPS for dy in group):
+            for chunk in together:
+                arrived = recv_ref.at[chunk, pl.ds(dy * Q, Q)]
+                pltpu.make_async_copy(arrived, arrived, recv_sem.at[chunk, dy]).wait()
+            part = nt_dot(
+                jnp.concatenate(
+                    [
+                        jnp.concatenate(
+                            [recv_ref[chunk, dy * Q + q] for q in range(Q)], axis=1
+                        )
+                        for chunk in together
+                    ],
+                    axis=0,
+                ),
+                spread_ref[dy],
+            )
+            volume = part if volume is None else volume + part
+        if together == TOGETHER[0]:
+            greeted(2)
+        for n, chunk in enumerate(together):
+            to_owners(chunk, volume[n * 2 * ROWS : (n + 1) * 2 * ROWS])
 
     tables[2].wait()
     pltpu.make_async_copy(zrecv_ref, zrecv_ref, zrecv_sem).wait()
@@ -432,6 +464,7 @@
             pltpu.SemaphoreType.DMA,
             pltpu.SemaphoreType.DMA((LOADS,)),
             pltpu.SemaphoreType.DMA((3,)),
+            pltpu.SemaphoreType.REGULAR((3,)),
         ],
         compiler_params=pltpu.CompilerParams(
             collective_id=0, has_side_effects=True, vmem_limit_bytes=55040 * 1024

time: 43.1 us -> 42.1 us (0.977); the launches traced: 42.4 us -> 42 us
  no operation moved by 1% of the time
where the time goes in v4:
time: 42.1 us; the launch traced here: 42 us
  Pallas kernels  40.6 us (96%)
  local copies, waits for them, and re-layouts  1.32 us (3%)
    pallas_call x1, Pallas kernels, on_device(): pl.pallas_call(insertion_kernel, out_shape=jax.ShapeDtypeStruct((2, J, NZ...  40.6 us

profile of v4, /device:TPU:1, one launch (start us, length us, event | category | flops | bytes accessed | tf_op | source)
XLA Modules:
  0.0 42.0 jit_solution(14447282566471354493)
XLA Ops:
  0.0 0.0 copy-start
  0.0 0.0 copy-start.1
  0.0 0.0 copy-start.2
  0.0 0.6 %copy-done = s32[128]{0:T(128)S(1)} copy-done((s32[128]{0:T(128)S(1)}, s32[128]{0:T(128)}, u32[]{:S(2)}) %copy-start) | copy-done | bytes 536
  0.7 0.0 copy-done.1
  0.7 0.0 copy-done.2
  0.7 40.6 %shard_map.73 = f32[2,8,512]{2,1,0:T(8,128)S(1)} custom-call(s32[1,128]{1,0:T(1,128)S(1)} %bitcast.7, s32[1,128]{1,0:T(1,128)S(1)} %bitcast.8, bf16[1,128]{1,0:T(2,128)(2,1)S(1)} %bitcast.9, bf16[128,2,4,512]{3,2,1,0:T(4,128)(2,1)} %images_hbm.1, bf16[4,256,512]{2,1,0:T(8,128)(2,1)} %constant.6.clone.xtab_hbm, bf16[2,512,8]{2,1,0:T(8,128)(2,1)} %constant.7.clone.xtap_hbm, ...), custom_call_target="tpu_custom_call" | custom-call | tf_op jit(solution)/shard_map/pallas_call | solution.py:438
  41.3 0.6 %copy.8 = f32[1,8,2,512]{3,2,1,0:T(2,128)} copy(f32[1,8,2,512]{3,1,2,0:T(8,128)S(1)} %bitcast.6) | data formatting | bytes 65536 | tf_op jit(solution)/shard_map/broadcast_in_dim | solution.py:481
Async XLA Ops:
  0.0 0.7 %copy-start = (s32[128]{0:T(128)S(1)}, s32[128]{0:T(128)}, u32[]{:S(2)}) copy-start(s32[128]{0:T(128)} %param.8) | copy-start | bytes 1540
  0.0 0.7 %copy-start.1 = (s32[128]{0:T(128)S(1)}, s32[128]{0:T(128)}, u32[]{:S(2)}) copy-start(s32[128]{0:T(128)} %param.9) | copy-start | bytes 1540
  0.0 0.7 %copy-start.2 = (bf16[128]{0:T(256)(128)(2,1)S(1)}, bf16[128]{0:T(256)(128)(2,1)}, u32[]{:S(2)}) copy-start(bf16[128]{0:T(256)(128)(2,1)} %param.10) | copy-start | bytes 772

commit v5 on v4

--- a/solution.py
+++ b/solution.py
@@ -307,9 +307,12 @@
             for across in ACROSS:
                 for dy in group:
                     send(chunk, dy, across)
-
-    greeted(0)
-    greet(1)
+        if chunk == 0:
+            greeted(0)
+            greet(1)
+
+    greeted(1)
+    greet(2)
 
     pltpu.make_async_copy(keys_ref, keys_ref, krecv_sem).wait()
     ztaps = tap_values(ZBINS)
@@ -341,10 +344,7 @@
                 block == jnp.bfloat16(b), pattern, jnp.bfloat16(0)
             )
 
-    pl.loop(0, PLANE // 2)(spread)
-    greeted(1)
-    greet(2)
-    pl.loop(PLANE // 2, PLANE)(spread)
+    pl.loop(0, PLANE)(spread)
 
     def to_owners(chunk, volume):
         for c in range(CLASSES):

time: 42.1 us -> 41.6 us (0.988)
  Pallas kernels: 40.6 us -> 40.1 us
    pallas_call x1, Pallas kernels: 40.6 us -> 40.1 us  [on_device(): pl.pallas_call(insertion_kernel, out_shape=jax.ShapeDtypeStruct((2, J, NZ...]
where the time goes in v5:
time: 41.6 us; the launch traced here: 41.5 us
  Pallas kernels  40.1 us (96%)
  local copies, waits for them, and re-layouts  1.32 us (3%)
    pallas_call x1, Pallas kernels, on_device(): pl.pallas_call(insertion_kernel, out_shape=jax.ShapeDtypeStruct((2, J, NZ...  40.1 us

profile of v5, /device:TPU:1, one launch (start us, length us, event | category | flops | bytes accessed | tf_op | source)
XLA Modules:
  0.0 41.5 jit_solution(9202661206584117740)
XLA Ops:
  0.0 0.0 copy-start
  0.0 0.0 copy-start.1
  0.0 0.0 copy-start.2
  0.0 0.6 %copy-done = s32[128]{0:T(128)S(1)} copy-done((s32[128]{0:T(128)S(1)}, s32[128]{0:T(128)}, u32[]{:S(2)}) %copy-start) | copy-done | bytes 536
  0.7 0.0 copy-done.1
  0.7 0.0 copy-done.2
  0.7 40.1 %shard_map.73 = f32[2,8,512]{2,1,0:T(8,128)S(1)} custom-call(s32[1,128]{1,0:T(1,128)S(1)} %bitcast.7, s32[1,128]{1,0:T(1,128)S(1)} %bitcast.8, bf16[1,128]{1,0:T(2,128)(2,1)S(1)} %bitcast.9, bf16[128,2,4,512]{3,2,1,0:T(4,128)(2,1)} %images_hbm.1, bf16[4,256,512]{2,1,0:T(8,128)(2,1)} %constant.6.clone.xtab_hbm, bf16[2,512,8]{2,1,0:T(8,128)(2,1)} %constant.7.clone.xtap_hbm, ...), custom_call_target="tpu_custom_call" | custom-call | tf_op jit(solution)/shard_map/pallas_call | solution.py:438
  40.8 0.6 %copy.8 = f32[1,8,2,512]{3,2,1,0:T(2,128)} copy(f32[1,8,2,512]{3,1,2,0:T(8,128)S(1)} %bitcast.6) | data formatting | bytes 65536 | tf_op jit(solution)/shard_map/broadcast_in_dim | solution.py:481
Async XLA Ops:
  0.0 0.7 %copy-start = (s32[128]{0:T(128)S(1)}, s32[128]{0:T(128)}, u32[]{:S(2)}) copy-start(s32[128]{0:T(128)} %param.8) | copy-start | bytes 1540
  0.0 0.7 %copy-start.1 = (s32[128]{0:T(128)S(1)}, s32[128]{0:T(128)}, u32[]{:S(2)}) copy-start(s32[128]{0:T(128)} %param.9) | copy-start | bytes 1540
  0.0 0.7 %copy-start.2 = (bf16[128]{0:T(256)(128)(2,1)S(1)}, bf16[128]{0:T(256)(128)(2,1)}, u32[]{:S(2)}) copy-start(bf16[128]{0:T(256)(128)(2,1)} %param.10) | copy-start | bytes 772

commit v6 on v5

--- a/solution.py
+++ b/solution.py
@@ -310,9 +310,9 @@
         if chunk == 0:
             greeted(0)
             greet(1)
-
-    greeted(1)
-    greet(2)
+        if chunk == 1:
+            greeted(1)
+            greet(2)
 
     pltpu.make_async_copy(keys_ref, keys_ref, krecv_sem).wait()
     ztaps = tap_values(ZBINS)

time: 41.6 us -> 42.3 us (1.017)
  Pallas kernels: 40.1 us -> 40.9 us
    pallas_call x1, Pallas kernels: 40.1 us -> 40.9 us  [on_device(): pl.pallas_call(insertion_kernel, out_shape=jax.ShapeDtypeStruct((2, J, NZ...]
where the time goes in v6:
time: 42.3 us; the launch traced here: 42.2 us
  Pallas kernels  40.9 us (97%)
  local copies, waits for them, and re-layouts  1.32 us (3%)
    pallas_call x1, Pallas kernels, on_device(): pl.pallas_call(insertion_kernel, out_shape=jax.ShapeDtypeStruct((2, J, NZ...  40.9 us

profile of v6, /device:TPU:1, one launch (start us, length us, event | category | flops | bytes accessed | tf_op | source)
XLA Modules:
  0.0 42.2 jit_solution(17401641570559307642)
XLA Ops:
  0.0 0.0 copy-start
  0.0 0.0 copy-start.1
  0.0 0.0 copy-start.2
  0.0 0.6 %copy-done = s32[128]{0:T(128)S(1)} copy-done((s32[128]{0:T(128)S(1)}, s32[128]{0:T(128)}, u32[]{:S(2)}) %copy-start) | copy-done | bytes 536
  0.7 0.0 copy-done.1
  0.7 0.0 copy-done.2
  0.7 40.9 %shard_map.73 = f32[2,8,512]{2,1,0:T(8,128)S(1)} custom-call(s32[1,128]{1,0:T(1,128)S(1)} %bitcast.7, s32[1,128]{1,0:T(1,128)S(1)} %bitcast.8, bf16[1,128]{1,0:T(2,128)(2,1)S(1)} %bitcast.9, bf16[128,2,4,512]{3,2,1,0:T(4,128)(2,1)} %images_hbm.1, bf16[4,256,512]{2,1,0:T(8,128)(2,1)} %constant.6.clone.xtab_hbm, bf16[2,512,8]{2,1,0:T(8,128)(2,1)} %constant.7.clone.xtap_hbm, ...), custom_call_target="tpu_custom_call" | custom-call | tf_op jit(solution)/shard_map/pallas_call | solution.py:438
  41.5 0.6 %copy.8 = f32[1,8,2,512]{3,2,1,0:T(2,128)} copy(f32[1,8,2,512]{3,1,2,0:T(8,128)S(1)} %bitcast.6) | data formatting | bytes 65536 | tf_op jit(solution)/shard_map/broadcast_in_dim | solution.py:481
Async XLA Ops:
  0.0 0.7 %copy-start = (s32[128]{0:T(128)S(1)}, s32[128]{0:T(128)}, u32[]{:S(2)}) copy-start(s32[128]{0:T(128)} %param.8) | copy-start | bytes 1540
  0.0 0.7 %copy-start.1 = (s32[128]{0:T(128)S(1)}, s32[128]{0:T(128)}, u32[]{:S(2)}) copy-start(s32[128]{0:T(128)} %param.9) | copy-start | bytes 1540
  0.0 0.7 %copy-start.2 = (bf16[128]{0:T(256)(128)(2,1)S(1)}, bf16[128]{0:T(256)(128)(2,1)}, u32[]{:S(2)}) copy-start(bf16[128]{0:T(256)(128)(2,1)} %param.10) | copy-start | bytes 772
